TPU v7x, 256 devices: a whole 4x4x8 slice. The times are simulated.
256 devices in a mesh: tile: 32 (over z_hi, y, core), lev: 8 (over x, z_lo).
Axes of the slice: x: 4, y: 4, z: 8 (z_hi: 4, z_lo: 2; z = z_hi * 2 + z_lo), core: 2. Of those that a mesh axis runs over, the one named last changes fastest.
Arguments:
- tracer_start: float32 [48, 2048, 720], P('lev', 'tile'), may hold values from -6 to 6
- wind_row: float32 [48, 2048, 720], P('lev', 'tile'), may hold values from -0.16 to 0.16
- wind_col: float32 [48, 2048, 720], P('lev', 'tile'), may hold values from -0.16 to 0.16
- diffusivity: float32 [48, 2048, 720], P('lev', 'tile'), may hold values from 0.01 to 0.16
- flux: float32 [11520, 128], P(('tile', 'lev')), may hold values from -6 to 6
- remap_weights: float32 [23040, 128, 128], P(('tile', 'lev')), may hold values from -0.5 to 0.5
- remap_tile: int32 [23040, 1], P(('tile', 'lev')), may hold values from 0 to 31; in each aligned block of 90 rows (0 to 89, 90 to 179, ...) at most 8 rows name the same one
- remap_block: int32 [23040], P(('tile', 'lev')), may hold values from 0 to 359
- profiles: float32 [64, 48], P(None, 'lev'), may hold values from -0.875 to 0.875
- sound_count: int32 [32], P('tile'), may hold values from 1 to 2048, 32768 in all
- sound_col: int32 [65536], P('tile'), may hold values from 0 to 46079
- sound_prof: int32 [65536], P('tile'), may hold values from 0 to 63
- sound_obs: float32 [65536], P('tile'), may hold values from -8 to 8
- sound_sigma: float32 [65536], P('tile'), may hold values from 0.5 to 2
Outputs:
- modeled: float32 [65536], P('tile')
- misfit: float32 [65536], P('tile')
- state_gradient: float32 [48, 2048, 720], P('lev', 'tile')
- flux_gradient: float32 [11520, 128], P(('tile', 'lev'))
Inputs may be any that keep to these rules, and one draw needn't show every extreme that they name: `remap_tile`: within the (90) entries of one device no tile is named more than 8 times, a bound that some block reaches. `sound_count`: some tile has exactly 2048 live soundings.
All inputs are finite; a program needn't handle non-finite values. No bound on the sum of `sound_count` on one device may be relied on, other than what follows from the above.
Results may differ from a plain program's by a relative error of at most 0.0003.
Values sent between devices are 32-bit elements; how exact they have to be, the bound alone decides.
A program may use at most 128 MiB of HBM per device.

v0:
```python
import jax
import jax.numpy as jnp
from jax import lax
from jax.sharding import PartitionSpec as P

highest = lax.Precision.HIGHEST


def with_halo(cells, sides, width):
    for axis, dim in sides:
        count = lax.axis_size(axis)
        ends = count - 1
        head = lax.slice_in_dim(cells, 0, width, axis=dim)
        tail = lax.slice_in_dim(cells, cells.shape[dim] - width, cells.shape[dim], axis=dim)
        cells = jnp.concatenate(
            [
                lax.ppermute(tail, axis, [(i, (i + 1) % count) for i in range(ends)]),
                cells,
                lax.ppermute(head, axis, [((i + 1) % count, i) for i in range(ends)]),
            ],
            axis=dim,
        )
    return cells


def from_behind(value, axis, steps):
    count = lax.axis_size(axis)
    leading, last = (max(0, -steps), min(count, count - steps))
    return lax.ppermute(value, axis, [(source, source + steps) for source in range(leading, last)])


def spread(block, axis, holder):
    block = jnp.where(lax.axis_index(axis) == holder, block, jnp.zeros_like(block))
    return lax.psum(block, axis)


def apply_step(field, above, below, upper, lower, coeffs, adjoint):
    rise, rise_low, cross, cross_left, mixing, mixing_low = coeffs
    right = jnp.roll(field, -1, axis=2)
    left = jnp.roll(field, 1, axis=2)
    rise_pos = jnp.maximum(rise, 0.0)
    rise_neg = jnp.minimum(rise, 0.0)
    low_pos = jnp.maximum(rise_low, 0.0)
    low_neg = jnp.minimum(rise_low, 0.0)
    cross_pos = jnp.maximum(cross, 0.0)
    cross_neg = jnp.minimum(cross, 0.0)
    left_pos = jnp.maximum(cross_left, 0.0)
    left_neg = jnp.minimum(cross_left, 0.0)
    diffusion = mixing * (above - field) - mixing_low * (field - below)
    if adjoint:
        rows_term = rise_pos * (upper - field) - low_neg * (lower - field)
        cols_term = cross_pos * (right - field) - left_neg * (left - field)
    else:
        rows_term = low_pos * lower + low_neg * field - rise_pos * field - rise_neg * upper
        cols_term = left_pos * left + left_neg * field - cross_pos * field - cross_neg * right
    return field + rows_term + cols_term + diffusion


def transport(field, coeffs, adjoint):
    padded = with_halo(field, (("tile", 1), ("lev", 0)), 1)
    above = padded[2:, 1:-1, :]
    below = padded[:-2, 1:-1, :]
    upper = padded[1:-1, 2:, :]
    lower = padded[1:-1, :-2, :]
    return apply_step(field, above, below, upper, lower, coeffs, adjoint)


def on_device(
    tracer_start,
    wind_row,
    wind_col,
    diffusivity,
    flux,
    remap_weights,
    remap_tile,
    remap_block,
    profiles,
    sound_count,
    sound_col,
    sound_prof,
    sound_obs,
    sound_sigma,
):
    levels, rows, cols = tracer_start.shape
    entries, block_size, flux_cells = remap_weights.shape
    blocks = rows * cols // block_size
    tiles = lax.axis_size("tile")
    tile_index = lax.axis_index("tile")
    lev_index = lax.axis_index("lev")
    row_ids = lax.broadcasted_iota(jnp.int32, (1, rows, 1), 1)
    top_row = (row_ids == rows - 1) & (tile_index == tiles - 1)
    rise = jnp.where(top_row, 0.0, wind_row)
    rise_edge = from_behind(rise[:, rows - 1, :], "tile", 1)
    rise_low = jnp.concatenate([rise_edge[:, None, :], rise[:, : rows - 1, :]], axis=1)
    level_ids = lax.broadcasted_iota(jnp.int32, (levels, 1, 1), 0)
    top_level = (level_ids == levels - 1) & (lev_index == lax.axis_size("lev") - 1)
    mixing = jnp.where(top_level, 0.0, diffusivity)
    mixing_edge = from_behind(mixing[levels - 1], "lev", 1)
    mixing_low = jnp.concatenate([mixing_edge[None], mixing[: levels - 1]], axis=0)
    cross_left = jnp.roll(wind_col, 1, axis=2)
    coeffs = (rise, rise_low, wind_col, cross_left, mixing, mixing_low)
    flux_rep = jnp.repeat(flux, 2, axis=0)
    contrib = jnp.einsum(
        "ecf,ef->ec", remap_weights, flux_rep, precision=highest, preferred_element_type=jnp.float32
    )
    target = remap_tile[:, 0]
    global_rows = target * blocks + remap_block
    count = lax.axis_size("tile") * blocks
    local = global_rows
    inside = (local >= 0) & (local < count)
    summed = jax.ops.segment_sum(contrib, jnp.where(inside, local, count), num_segments=count + 1)
    partial_value = lax.psum_scatter(summed[:count], "tile", scatter_dimension=0, tiled=True)
    state = transport(tracer_start, coeffs, False)
    surface = lax.psum(partial_value, "lev").reshape(rows, cols)
    emission = jnp.where(lev_index == 0, surface, 0.0)
    state = state.at[0].add(emission)
    state = transport(state, coeffs, False)
    state = state.at[0].add(emission)
    slots = sound_col.shape[0]
    live = lax.iota(jnp.int32, slots) < sound_count[0]
    chooser = (sound_prof[:, None] == lax.iota(jnp.int32, profiles.shape[0])[None, :]).astype(
        jnp.float32
    )
    weights = jnp.dot(chooser, profiles, precision=highest, preferred_element_type=jnp.float32)
    flat = state.reshape(levels, rows * cols)
    values = jnp.take(flat, sound_col, axis=1)
    partial_column = jnp.sum(weights * values.T, axis=1)
    column = lax.psum(partial_column, "lev")
    modeled = jnp.where(live, column, 0.0)
    scaled = (column - sound_obs) / sound_sigma
    size_abs = jnp.abs(scaled)
    huber = jnp.where(size_abs <= 1.0, 0.5 * scaled * scaled, size_abs - 0.5)
    misfit = jnp.where(live, huber, 0.0)
    slope = jnp.where(live, jnp.clip(scaled, -1.0, 1.0) / sound_sigma, 0.0)
    adjoint_two = (
        jnp.zeros((levels, rows * cols), jnp.float32)
        .at[:, sound_col]
        .add((weights * slope[:, None]).T)
    )
    adjoint_two = adjoint_two.reshape(levels, rows, cols)
    adjoint_one = transport(adjoint_two, coeffs, True)
    surface_bar = (adjoint_two[0] + adjoint_one[0]).reshape(blocks, block_size)
    shared = spread(surface_bar, "lev", 0)
    piece = lax.all_gather(shared, "tile", axis=0, tiled=True)
    local = global_rows
    inside = (local >= 0) & (local < piece.shape[0])
    found = piece[jnp.clip(local, 0, piece.shape[0] - 1)]
    picked = jnp.where(inside[:, None], found, 0.0)
    state_gradient = transport(adjoint_one, coeffs, True)
    per_entry = jnp.einsum(
        "ecf,ec->ef", remap_weights, picked, precision=highest, preferred_element_type=jnp.float32
    )
    flux_gradient = per_entry.reshape(-1, 2, flux_cells).sum(axis=1)
    return (modeled, misfit, state_gradient, flux_gradient)


def solution(mesh):
    in_specs = (
        P("lev", "tile", None),
        P("lev", "tile", None),
        P("lev", "tile", None),
        P("lev", "tile", None),
        P(("tile", "lev"), None),
        P(("tile", "lev"), None, None),
        P(("tile", "lev"), None),
        P(("tile", "lev")),
        P(None, "lev"),
        P("tile"),
        P("tile"),
        P("tile"),
        P("tile"),
        P("tile"),
    )
    out_specs = (P("tile"), P("tile"), P("lev", "tile", None), P(("tile", "lev"), None))
    return jax.shard_map(
        on_device, mesh=mesh, in_specs=in_specs, out_specs=out_specs, check_vma=False
    )
```

profile of v0, /device:TPU:1, one launch (start us, length us, event | category | flops | bytes accessed | tf_op | source)
XLA Modules:
  0.0 527.5 jit_solution(2005856209609383764)
XLA Ops:
  8.4 11.2 %fusion.93 = f32[90,1,128]{2,1,0:T(1,128)S(1)} fusion(f32[90,128,128]{2,1,0:T(8,128)} %param.23, f32[90,128,1]{1,2,0:T(1,128)S(1)} %bitcast.55), kind=kOutput, calls=%fused_computation.180 | convolution fusion | flops 17694720 | bytes 5990400 | tf_op jit(solution)/shard_map/ecf,ef->ec/dot_general | solution.py:103
  19.6 3.8 scatter_custom_fusion
  23.3 4.5 slice.304
  29.6 4.6 collective-permute-start.1
  36.9 3.3 collective-permute-start
  41.1 3.5 collective-permute-start.4
  50.1 4.0 collective-permute-start.5
  57.8 76.1 %reduce-scatter.4.cloned.1.call-done = f32[360,128]{1,0:T(8,128)} async-done(((f32[11520,128]{1,0:T(8,128)}), f32[360,128]{1,0:T(8,128)}) %reduce-scatter.4.cloned.1.call-update) | async-done | bytes 184336
  134.9 6.5 %fusion.46 = f32[6,64,720]{2,1,0:T(8,128)S(1)} fusion(f32[6,64,720]{2,1,0:T(8,128)} %param.18, f32[1,66,720]{2,1,0:T(8,128)} %copy-done.30, f32[6,1,720]{2,1,0:T(1,128)} %collective-permute-done.2, f32[6,1,720]{2,1,0:T(1,128)} %collective-permute-done.1, f32[1,66,720]{2,1,0:T(8,128)} %copy-done.29, f32[6,64,719]{2,1,0:T(8,128)} %get-tuple-element.55, ...), kind=kLoop, calls=%fused_computation.76 | loop fusion | flops 12441600 | bytes 11473990 | tf_op jit(solution)/shard_map/add | solution.py:56
  141.4 67.9 %all-reduce.4.cloned.1.call-done = f32[360,128]{1,0:T(8,128)} async-done(((f32[360,128]{1,0:T(8,128)}), f32[360,128]{1,0:T(8,128)}) %all-reduce.4.cloned.1.call-update) | async-done | bytes 184336 | tf_op jit(solution)/shard_map/psum | solution.py:114
  213.7 9.0 %collective-permute-start.6 = (f32[6,1,720]{2,1,0:T(1,128)S(1)}, f32[6,1,720]{2,1,0:T(1,128)S(1)}, u32[]{:S(2)}, u32[]{:S(2)}) collective-permute-start(f32[6,1,720]{2,1,0:T(1,128)S(1)} %get-tuple-element.52), channel_id=1, source_target_pairs={{0,8},{8,16},{16,24},{24,32},{32,40},{40,48},{48,56},{56,64},{64,7... | collective-permute-start | bytes 51848 | tf_op jit(solution)/shard_map/ppermute | solution.py:17
  225.1 2.7 collective-permute-done.7
  229.1 4.0 collective-permute-start.9
  233.2 3.6 collective-permute-done.8
  237.1 3.6 fusion.33
  242.3 11.9 %copy.79 = f32[6,64,720]{0,2,1:T(8,128)} copy(f32[6,64,720]{2,1,0:T(8,128)} %fusion.70) | data formatting | bytes 2211840 | tf_op jit(solution)/shard_map/scatter-add | solution.py:118
  254.3 13.2 %gather_fusion = f32[2048,6]{1,0:T(8,128)S(1)} fusion(f32[6,46080]{0,1:T(8,128)} %bitcast.49, s32[2048]{0:T(1024)S(1)} %get-tuple-element.64), kind=kCustom, calls=%fused_computation | custom fusion | bytes 106496 | tf_op jit(solution)/shard_map/jit(_take)/gather | solution.py:126
  268.8 15.9 %psum.22 = f32[2048]{0:T(1024)S(1)} all-reduce(f32[2048]{0:T(1024)S(1)} %get-tuple-element.67), channel_id=1, replica_groups=mesh['tile'=32,'lev'=8] {'lev'}, use_global_device_ids=true, to_apply=%region_4.5 | all-reduce | flops 2048 | bytes 16384 | tf_op jit(solution)/shard_map/psum | solution.py:128
  285.8 20.8 %scatter_custom_fusion.1 = f32[6,46080]{0,1:T(8,128)} fusion(s32[2048]{0:T(1024)} %get-tuple-element.63, f32[2048,6]{1,0:T(8,128)S(1)} %copy.81, f32[]{:T(128)} %constant.93.clone.1), kind=kCustom, calls=%fused_computation.5 | custom fusion | flops 12288 | bytes 1106432 | tf_op jit(solution)/shard_map/scatter-add | solution.py:138
  306.6 11.9 %slice_reduce_fusion = f32[46080]{0:T(1024)} fusion(f32[6,46080]{0,1:T(8,128)} %scatter_custom_fusion.1), kind=kLoop, calls=%fused_computation.4 | loop fusion | bytes 368640 | tf_op jit(solution)/shard_map/slice | solution.py:142
  318.5 12.5 %copy.88 = f32[6,64,720]{2,1,0:T(8,128)S(1)} copy(f32[6,64,720]{0,2,1:T(8,128)} %bitcast.40) | data formatting | bytes 2211840 | tf_op jit(solution)/shard_map/reshape | solution.py:140
  331.1 7.2 %collective-permute-start.11 = (f32[6,1,720]{2,1,0:T(1,128)S(1)}, f32[6,1,720]{2,1,0:T(1,128)S(1)}, u32[]{:S(2)}, u32[]{:S(2)}) collective-permute-start(f32[6,1,720]{2,1,0:T(1,128)S(1)} %get-tuple-element.46), channel_id=1, source_target_pairs={{0,8},{8,16},{16,24},{24,32},{32,40},{40,48},{48,56},{56,64},{64,7... | collective-permute-start | bytes 51848 | tf_op jit(solution)/shard_map/ppermute | solution.py:17
  344.8 4.0 collective-permute-start.13
  348.9 3.2 collective-permute-done.12
  357.2 78.0 %all-reduce.6.cloned.1.call-done = f32[360,128]{1,0:T(8,128)} async-done(((f32[360,128]{1,0:T(8,128)}), f32[360,128]{1,0:T(8,128)}) %all-reduce.6.cloned.1.call-update) | async-done | bytes 184336 | tf_op jit(solution)/shard_map/psum | solution.py:34
  435.3 9.0 %collective-permute-start.15 = (f32[6,1,720]{2,1,0:T(1,128)S(1)}, f32[6,1,720]{2,1,0:T(1,128)S(1)}, u32[]{:S(2)}, u32[]{:S(2)}) collective-permute-start(f32[6,1,720]{2,1,0:T(1,128)S(1)} %get-tuple-element.40), channel_id=1, source_target_pairs={{0,8},{8,16},{16,24},{24,32},{32,40},{40,48},{48,56},{56,64},{64,7... | collective-permute-start | bytes 51848 | tf_op jit(solution)/shard_map/ppermute | solution.py:17
  450.7 4.2 collective-permute-start.17
  455.1 5.8 %collective-permute-done.16 = f32[1,66,720]{2,1,0:T(8,128)S(1)} collective-permute-done((f32[1,66,720]{2,1,0:T(8,128)S(1)}, f32[1,66,720]{2,1,0:T(8,128)S(1)}, u32[]{:S(2)}, u32[]{:S(2)}) %collective-permute-start.16) | collective-permute-done | bytes 190112 | tf_op jit(solution)/shard_map/ppermute | solution.py:19
  460.9 3.3 fusion.7
  464.2 45.7 %all-gather.2.cloned.1.call-done = f32[11520,128]{1,0:T(8,128)} async-done(((f32[360,128]{1,0:T(8,128)}), f32[11520,128]{1,0:T(8,128)}) %all-gather.2.cloned.1.call-update) | async-done | bytes 5898256 | tf_op jit(solution)/shard_map/all_gather | solution.py:144
  509.9 3.3 gather_fusion.1
  513.3 7.0 %fusion.76 = f32[90,1,128]{2,1,0:T(1,128)S(1)} fusion(f32[90,128,128]{2,1,0:T(8,128)} %param.23, f32[90,128,1]{1,0,2:T(8,128)S(1)} %select_bitcast_fusion), kind=kOutput, calls=%fused_computation.147 | convolution fusion | flops 17694720 | bytes 5990400 | tf_op jit(solution)/shard_map/ecf,ec->ef/dot_general | solution.py:150
  (159 shorter events, 47.0 us)
Async XLA Ops:
  7.2 126.8 %reduce-scatter.4.cloned.1.call-start = ((), (), s32[]{:S(2)}) async-start(), calls=%async_computation.4 | async-start | bytes 6082560
  27.9 181.4 %all-reduce.4.cloned.1.call-start = ((), (), s32[]{:S(2)}) async-start(), calls=%async_computation.1 | async-start | bytes 368640 | tf_op jit(solution)/shard_map/psum | solution.py:114
  29.6 18.2 %collective-permute-start.1 = (f32[6,1,720]{2,1,0:T(1,128)}, f32[6,1,720]{2,1,0:T(1,128)}, u32[]{:S(2)}, u32[]{:S(2)}) collective-permute-start(f32[6,1,720]{2,1,0:T(1,128)} %get-tuple-element.58), channel_id=1, source_target_pairs={{0,8},{8,16},{16,24},{24,32},{32,40},{40,48},{48,56},{56,64},{64,7... | collective-permute-start | bytes 51848 | tf_op jit(solution)/shard_map/ppermute | solution.py:17
  34.2 13.7 %collective-permute-start.2 = (f32[6,1,720]{2,1,0:T(1,128)}, f32[6,1,720]{2,1,0:T(1,128)}, u32[]{:S(2)}, u32[]{:S(2)}) collective-permute-start(f32[6,1,720]{2,1,0:T(1,128)} %get-tuple-element.59), channel_id=1, source_target_pairs={{8,0},{16,8},{24,16},{32,24},{40,32},{48,40},{56,48},{64,56},{72,6... | collective-permute-start | bytes 51848 | tf_op jit(solution)/shard_map/ppermute | solution.py:19
  36.8 200.3 %copy-start.3 = (f32[6,64,720]{2,1,0:T(8,128)}, f32[6,64,720]{2,1,0:T(8,128)S(1)}, u32[]{:S(2)}) copy-start(f32[6,64,720]{2,1,0:T(8,128)S(1)} %broadcast_select_fusion.1) | copy-start | bytes 3317764
  36.9 20.3 %collective-permute-start = (f32[6,720]{1,0:T(8,128)S(1)}, f32[6,720]{1,0:T(8,128)S(1)}, u32[]{:S(2)}, u32[]{:S(2)}) collective-permute-start(f32[6,720]{1,0:T(8,128)S(1)} %bitcast.56), channel_id=1, source_target_pairs={{0,8},{8,16},{16,24},{24,32},{32,40},{40,48},{48,56},{56,64},{64,7... | collective-permute-start | bytes 51848 | tf_op jit(solution)/shard_map/ppermute | solution.py:29
  41.1 92.9 %collective-permute-start.4 = (f32[64,720]{1,0:T(8,128)}, f32[64,720]{1,0:T(8,128)S(1)}, u32[]{:S(2)}, u32[]{:S(2)}) collective-permute-start(f32[64,720]{1,0:T(8,128)} %slice_bitcast_fusion), channel_id=1, source_target_pairs={{0,1},{1,2},{2,3},{3,4},{4,5},{5,6},{6,7},{8,9},{9,10},{10,11},{11... | collective-permute-start | bytes 552968 | tf_op jit(solution)/shard_map/ppermute | solution.py:29
  48.7 85.4 %collective-permute-start.3 = (f32[1,66,720]{2,1,0:T(8,128)S(1)}, f32[1,66,720]{2,1,0:T(8,128)S(1)}, u32[]{:S(2)}, u32[]{:S(2)}) collective-permute-start(f32[1,66,720]{2,1,0:T(8,128)S(1)} %get-tuple-element.34), channel_id=1, source_target_pairs={{1,0},{2,1},{3,2},{4,3},{5,4},{6,5},{7,6},{9,8},{10,9},{11,10},{12... | collective-permute-start | bytes 570248 | tf_op jit(solution)/shard_map/ppermute | solution.py:19
  50.1 84.0 %collective-permute-start.5 = (f32[1,66,720]{2,1,0:T(8,128)S(1)}, f32[1,66,720]{2,1,0:T(8,128)S(1)}, u32[]{:S(2)}, u32[]{:S(2)}) collective-permute-start(f32[1,66,720]{2,1,0:T(8,128)S(1)} %get-tuple-element.35), channel_id=1, source_target_pairs={{0,1},{1,2},{2,3},{3,4},{4,5},{5,6},{6,7},{8,9},{9,10},{10,11},{11... | collective-permute-start | bytes 570248 | tf_op jit(solution)/shard_map/ppermute | solution.py:17
  134.0 301.2 %all-reduce.6.cloned.1.call-start = ((), (), s32[]{:S(2)}) async-start(), calls=%async_computation.2 | async-start | bytes 368640 | tf_op jit(solution)/shard_map/psum | solution.py:34
  213.7 11.4 %collective-permute-start.6 = (f32[6,1,720]{2,1,0:T(1,128)S(1)}, f32[6,1,720]{2,1,0:T(1,128)S(1)}, u32[]{:S(2)}, u32[]{:S(2)}) collective-permute-start(f32[6,1,720]{2,1,0:T(1,128)S(1)} %get-tuple-element.52), channel_id=1, source_target_pairs={{0,8},{8,16},{16,24},{24,32},{32,40},{40,48},{48,56},{56,64},{64,7... | collective-permute-start | bytes 51848 | tf_op jit(solution)/shard_map/ppermute | solution.py:17
  222.7 5.1 collective-permute-start.7
  227.8 9.0 %collective-permute-start.8 = (f32[1,66,720]{2,1,0:T(8,128)S(1)}, f32[1,66,720]{2,1,0:T(8,128)S(1)}, u32[]{:S(2)}, u32[]{:S(2)}) collective-permute-start(f32[1,66,720]{2,1,0:T(8,128)S(1)} %get-tuple-element.32), channel_id=1, source_target_pairs={{1,0},{2,1},{3,2},{4,3},{5,4},{6,5},{7,6},{9,8},{10,9},{11,10},{12... | collective-permute-start | bytes 570248 | tf_op jit(solution)/shard_map/ppermute | solution.py:19
  229.1 8.0 %collective-permute-start.9 = (f32[1,66,720]{2,1,0:T(8,128)S(1)}, f32[1,66,720]{2,1,0:T(8,128)S(1)}, u32[]{:S(2)}, u32[]{:S(2)}) collective-permute-start(f32[1,66,720]{2,1,0:T(8,128)S(1)} %get-tuple-element.33), channel_id=1, source_target_pairs={{0,1},{1,2},{2,3},{3,4},{4,5},{5,6},{6,7},{8,9},{9,10},{10,11},{11... | collective-permute-start | bytes 570248 | tf_op jit(solution)/shard_map/ppermute | solution.py:17
  254.3 30.5 %copy-start.32 = (f32[2048]{0:T(1024)S(1)}, f32[2048]{0:T(1024)}, u32[]{:S(2)}) copy-start(f32[2048]{0:T(1024)} %param.31) | copy-start | bytes 24580
  254.3 30.5 %copy-start.33 = (f32[2048]{0:T(1024)S(1)}, f32[2048]{0:T(1024)}, u32[]{:S(2)}) copy-start(f32[2048]{0:T(1024)} %param.30) | copy-start | bytes 24580
  331.1 9.6 %collective-permute-start.11 = (f32[6,1,720]{2,1,0:T(1,128)S(1)}, f32[6,1,720]{2,1,0:T(1,128)S(1)}, u32[]{:S(2)}, u32[]{:S(2)}) collective-permute-start(f32[6,1,720]{2,1,0:T(1,128)S(1)} %get-tuple-element.46), channel_id=1, source_target_pairs={{0,8},{8,16},{16,24},{24,32},{32,40},{40,48},{48,56},{56,64},{64,7... | collective-permute-start | bytes 51848 | tf_op jit(solution)/shard_map/ppermute | solution.py:17
  338.4 5.1 collective-permute-start.10
  343.5 8.6 %collective-permute-start.12 = (f32[1,66,720]{2,1,0:T(8,128)S(1)}, f32[1,66,720]{2,1,0:T(8,128)S(1)}, u32[]{:S(2)}, u32[]{:S(2)}) collective-permute-start(f32[1,66,720]{2,1,0:T(8,128)S(1)} %get-tuple-element.30), channel_id=1, source_target_pairs={{1,0},{2,1},{3,2},{4,3},{5,4},{6,5},{7,6},{9,8},{10,9},{11,10},{12... | collective-permute-start | bytes 570248 | tf_op jit(solution)/shard_map/ppermute | solution.py:19
  344.8 8.0 %collective-permute-start.13 = (f32[1,66,720]{2,1,0:T(8,128)S(1)}, f32[1,66,720]{2,1,0:T(8,128)S(1)}, u32[]{:S(2)}, u32[]{:S(2)}) collective-permute-start(f32[1,66,720]{2,1,0:T(8,128)S(1)} %get-tuple-element.31), channel_id=1, source_target_pairs={{0,1},{1,2},{2,3},{3,4},{4,5},{5,6},{6,7},{8,9},{9,10},{10,11},{11... | collective-permute-start | bytes 570248 | tf_op jit(solution)/shard_map/ppermute | solution.py:17
  355.3 79.9 %copy-start.35 = (s32[90]{0:T(128)S(1)}, s32[90]{0:T(128)}, u32[]{:S(2)}) copy-start(s32[90]{0:T(128)} %get-tuple-element.65) | copy-start | bytes 1084
  355.3 80.0 %copy-start.36 = (s32[90]{0:T(128)S(1)}, s32[90]{0:T(128)}, u32[]{:S(2)}) copy-start(s32[90]{0:T(128)} %param.25) | copy-start | bytes 1084
  355.3 80.0 %copy-start.37 = (s32[90,1]{0,1:T(1,128)S(1)}, s32[90,1]{0,1:T(1,128)}, u32[]{:S(2)}) copy-start(s32[90,1]{0,1:T(1,128)} %param.24) | copy-start | bytes 1084
  357.2 152.7 %all-gather.2.cloned.1.call-start = ((), (), s32[]{:S(2)}) async-start(), calls=%async_computation.3 | async-start | bytes 6082560 | tf_op jit(solution)/shard_map/all_gather | solution.py:144
  435.3 11.4 %collective-permute-start.15 = (f32[6,1,720]{2,1,0:T(1,128)S(1)}, f32[6,1,720]{2,1,0:T(1,128)S(1)}, u32[]{:S(2)}, u32[]{:S(2)}) collective-permute-start(f32[6,1,720]{2,1,0:T(1,128)S(1)} %get-tuple-element.40), channel_id=1, source_target_pairs={{0,8},{8,16},{16,24},{24,32},{32,40},{40,48},{48,56},{56,64},{64,7... | collective-permute-start | bytes 51848 | tf_op jit(solution)/shard_map/ppermute | solution.py:17
  444.3 5.1 collective-permute-start.14
  446.2 14.6 %copy-start.13 = (f32[6,64,720]{2,1,0:T(8,128)S(1)}, f32[6,64,720]{2,1,0:T(8,128)}, u32[]{:S(2)}) copy-start(f32[6,64,720]{2,1,0:T(8,128)} %param.19) | copy-start | bytes 3317764
  446.3 14.6 %copy-start.16 = (f32[5,64,720]{2,1,0:T(8,128)S(1)}, f32[5,64,720]{2,1,0:T(8,128)}, u32[]{:S(2)}) copy-start(f32[5,64,720]{2,1,0:T(8,128)} %slice.302) | copy-start | bytes 2764804
  446.3 14.6 %copy-start.20 = (f32[6,64,1]{2,1,0:T(8,128)S(1)}, f32[6,64,1]{2,1,0:T(8,128)}, u32[]{:S(2)}) copy-start(f32[6,64,1]{2,1,0:T(8,128)} %slice.242) | copy-start | bytes 4612
  446.3 14.6 %copy-start.24 = (f32[64,720]{1,0:T(8,128)S(1)}, f32[64,720]{1,0:T(8,128)}, u32[]{:S(2)}) copy-start(f32[64,720]{1,0:T(8,128)} %copy-done.21) | copy-start | bytes 552964
  449.4 11.4 %collective-permute-start.16 = (f32[1,66,720]{2,1,0:T(8,128)S(1)}, f32[1,66,720]{2,1,0:T(8,128)S(1)}, u32[]{:S(2)}, u32[]{:S(2)}) collective-permute-start(f32[1,66,720]{2,1,0:T(8,128)S(1)} %get-tuple-element.28), channel_id=1, source_target_pairs={{1,0},{2,1},{3,2},{4,3},{5,4},{6,5},{7,6},{9,8},{10,9},{11,10},{12... | collective-permute-start | bytes 570248 | tf_op jit(solution)/shard_map/ppermute | solution.py:19
  450.7 10.1 %collective-permute-start.17 = (f32[1,66,720]{2,1,0:T(8,128)S(1)}, f32[1,66,720]{2,1,0:T(8,128)S(1)}, u32[]{:S(2)}, u32[]{:S(2)}) collective-permute-start(f32[1,66,720]{2,1,0:T(8,128)S(1)} %get-tuple-element.29), channel_id=1, source_target_pairs={{0,1},{1,2},{2,3},{3,4},{4,5},{5,6},{6,7},{8,9},{9,10},{10,11},{11... | collective-permute-start | bytes 570248 | tf_op jit(solution)/shard_map/ppermute | solution.py:17
  (30 other events, 284.1 us)
Sparse Core Ops, SparseCore 0:
  28.0 105.9 reduce-scatter.3
  136.6 72.6 all-reduce.3
  357.3 77.8 all-reduce.5
  437.7 72.1 all-gather.1
where the time goes:
time: 529 us; the launch traced here: 527 us
  waiting for transfers between devices  289 us (55%)
  local copies, waits for them, and re-layouts  70.2 us (13%)
  starting transfers between devices  66.4 us (13%)
  other arithmetic  51.3 us (10%)
  matrix products  19.1 us (4%)
  blocking collectives  15.9 us (3%)
  between operations  15.3 us (3%)
    psum x1, waiting for transfers between devices, spread(): return lax.psum(block, axis)  78 us
    unnamed x5, waiting for transfers between devices  76.2 us
    psum x1, waiting for transfers between devices, on_device(): surface = lax.psum(partial_value, 'lev').reshape(rows, cols)  67.9 us
    ppermute x8, starting transfers between devices, with_halo(): lax.ppermute(tail, axis, [(i, (i + 1) % count) for i in range(ends)])  46 us
    all_gather x1, waiting for transfers between devices, on_device(): piece = lax.all_gather(shared, 'tile', axis=0, tiled=True)  45.7 us
    scatter-add x1, other arithmetic, on_device(): adjoint_two = jnp.zeros((levels, rows * cols), jnp.float32).at[:, sound_c...  20.8 us
    ppermute x8, waiting for transfers between devices, with_halo(): lax.ppermute(head, axis, [((i + 1) % count, i) for i in range(ends)])  20.6 us
    psum x1, blocking collectives, on_device(): column = lax.psum(partial_column, 'lev')  15.9 us
  transfers between devices with their start and end apart: 22, of which 12 were waited for; matrix products, arithmetic and copies ran while one was open for 4% of the time, Pallas kernels for 0%

commit v1 on v0

--- a/solution.py
+++ b/solution.py
@@ -111,7 +111,7 @@
     summed = jax.ops.segment_sum(contrib, jnp.where(inside, local, count), num_segments=count + 1)
     partial_value = lax.psum_scatter(summed[:count], "tile", scatter_dimension=0, tiled=True)
     state = transport(tracer_start, coeffs, False)
-    surface = lax.psum(partial_value, "lev").reshape(rows, cols)
+    surface = jnp.sum(lax.all_gather(partial_value, "lev"), axis=0).reshape(rows, cols)
     emission = jnp.where(lev_index == 0, surface, 0.0)
     state = state.at[0].add(emission)
     state = transport(state, coeffs, False)

time: 529 us -> 504 us (0.953)
  waiting for transfers between devices: 289 us -> 267 us
    psum x1 -> x0, waiting for transfers between devices: 67.9 us -> none  [on_device(): surface = lax.psum(partial_value, 'lev').reshape(rows, cols)]
    unnamed x5, waiting for transfers between devices: 76.2 us -> 97.4 us
    all_gather x0 -> x1, waiting for transfers between devices: none -> 17.7 us  [on_device(): lax.all_gather(partial_value, 'lev')]
    ppermute x8, waiting for transfers between devices: 20.6 us -> 27.6 us  [with_halo(): lax.ppermute(head, axis, [((i + 1) % count, i) for i in range(ends)])]
  transfers between devices with their start and end apart: 22 -> 22, of which waited for: 12 -> 13; matrix products, arithmetic and copies ran while one was open for 4% -> 4% of each run, Pallas kernels for 0% -> 0%
where the time goes in v1:
time: 504 us; the launch traced here: 503 us
  waiting for transfers between devices  267 us (53%)
  local copies, waits for them, and re-layouts  68.8 us (14%)
  starting transfers between devices  62.2 us (12%)
  other arithmetic  53.7 us (11%)
  matrix products  19.1 us (4%)
  blocking collectives  17.3 us (3%)
  between operations  15.3 us (3%)
    unnamed x5, waiting for transfers between devices  97.4 us
    psum x1, waiting for transfers between devices, spread(): return lax.psum(block, axis)  77.1 us
    all_gather x1, waiting for transfers between devices, on_device(): piece = lax.all_gather(shared, 'tile', axis=0, tiled=True)  45.7 us
    ppermute x8, starting transfers between devices, with_halo(): lax.ppermute(tail, axis, [(i, (i + 1) % count) for i in range(ends)])  42.2 us
    ppermute x8, waiting for transfers between devices, with_halo(): lax.ppermute(head, axis, [((i + 1) % count, i) for i in range(ends)])  27.6 us
    scatter-add x1, other arithmetic, on_device(): adjoint_two = jnp.zeros((levels, rows * cols), jnp.float32).at[:, sound_c...  20.8 us
    all_gather x1, waiting for transfers between devices, on_device(): lax.all_gather(partial_value, 'lev')  17.7 us
    psum x1, blocking collectives, on_device(): column = lax.psum(partial_column, 'lev')  17.3 us
  transfers between devices with their start and end apart: 22, of which 13 were waited for; matrix products, arithmetic and copies ran while one was open for 4% of the time, Pallas kernels for 0%

profile of v1, /device:TPU:1, one launch (start us, length us, event | category | flops | bytes accessed | tf_op | source)
XLA Modules:
  0.0 503.0 jit_solution(5778655687447561828)
XLA Ops:
  8.5 11.2 %fusion.93 = f32[90,1,128]{2,1,0:T(1,128)S(1)} fusion(f32[90,128,128]{2,1,0:T(8,128)} %param.23, f32[90,128,1]{1,2,0:T(1,128)S(1)} %bitcast.57), kind=kOutput, calls=%fused_computation.180 | convolution fusion | flops 17694720 | bytes 5990400 | tf_op jit(solution)/shard_map/ecf,ef->ec/dot_general | solution.py:103
  19.6 3.8 scatter_custom_fusion
  23.4 4.5 slice.304
  29.7 4.6 collective-permute-start.1
  36.7 97.3 %reduce-scatter.4.cloned.1.call-done = f32[360,128]{1,0:T(8,128)} async-done(((f32[11520,128]{1,0:T(8,128)}), f32[360,128]{1,0:T(8,128)}) %reduce-scatter.4.cloned.1.call-update) | async-done | bytes 184336
  134.3 4.4 collective-permute-start
  147.0 4.9 collective-permute-start.5
  154.4 6.4 %collective-permute-done.3 = f32[1,66,720]{2,1,0:T(8,128)S(1)} collective-permute-done((f32[1,66,720]{2,1,0:T(8,128)S(1)}, f32[1,66,720]{2,1,0:T(8,128)S(1)}, u32[]{:S(2)}, u32[]{:S(2)}) %collective-permute-start.3) | collective-permute-done | bytes 190112 | tf_op jit(solution)/shard_map/ppermute | solution.py:19
  162.4 6.7 %fusion.46 = f32[6,64,720]{2,1,0:T(8,128)S(1)} fusion(f32[6,64,720]{2,1,0:T(8,128)} %param.18, f32[1,66,720]{2,1,0:T(8,128)} %copy-done.32, f32[6,1,720]{2,1,0:T(1,128)} %collective-permute-done.2, f32[6,1,720]{2,1,0:T(1,128)} %collective-permute-done.1, f32[1,66,720]{2,1,0:T(8,128)} %copy-done.31, f32[6,64,719]{2,1,0:T(8,128)} %get-tuple-element.55, ...), kind=kLoop, calls=%fused_computation.76 | loop fusion | flops 12441600 | bytes 11473990 | tf_op jit(solution)/shard_map/add | solution.py:56
  169.1 17.7 %all-gather.6.cloned.1.call-done = f32[2880,128]{1,0:T(8,128)} async-done(((f32[360,128]{1,0:T(8,128)}), f32[2880,128]{1,0:T(8,128)}) %all-gather.6.cloned.1.call-update) | async-done | bytes 1474576 | tf_op jit(solution)/shard_map/all_gather | solution.py:114
  193.3 3.9 collective-permute-start.6
  199.6 2.7 collective-permute-done.7
  203.6 4.0 collective-permute-start.9
  207.7 3.6 collective-permute-done.8
  211.6 3.6 fusion.33
  216.8 11.9 %copy.79 = f32[6,64,720]{0,2,1:T(8,128)} copy(f32[6,64,720]{2,1,0:T(8,128)} %fusion.70) | data formatting | bytes 2211840 | tf_op jit(solution)/shard_map/scatter-add | solution.py:118
  228.8 13.2 %gather_fusion = f32[2048,6]{1,0:T(8,128)S(1)} fusion(f32[6,46080]{0,1:T(8,128)} %bitcast.50, s32[2048]{0:T(1024)S(1)} %get-tuple-element.64), kind=kCustom, calls=%fused_computation | custom fusion | bytes 106496 | tf_op jit(solution)/shard_map/jit(_take)/gather | solution.py:126
  243.3 17.3 %psum.14 = f32[2048]{0:T(1024)S(1)} all-reduce(f32[2048]{0:T(1024)S(1)} %get-tuple-element.67), channel_id=1, replica_groups=mesh['tile'=32,'lev'=8] {'lev'}, use_global_device_ids=true, to_apply=%region_4.5 | all-reduce | flops 2048 | bytes 16384 | tf_op jit(solution)/shard_map/psum | solution.py:128
  261.6 20.8 %scatter_custom_fusion.1 = f32[6,46080]{0,1:T(8,128)} fusion(s32[2048]{0:T(1024)} %get-tuple-element.63, f32[2048,6]{1,0:T(8,128)S(1)} %copy.81, f32[]{:T(128)} %constant.93.clone.1), kind=kCustom, calls=%fused_computation.5 | custom fusion | flops 12288 | bytes 1106432 | tf_op jit(solution)/shard_map/scatter-add | solution.py:138
  282.5 11.9 %slice_reduce_fusion = f32[46080]{0:T(1024)} fusion(f32[6,46080]{0,1:T(8,128)} %scatter_custom_fusion.1), kind=kLoop, calls=%fused_computation.4 | loop fusion | bytes 368640 | tf_op jit(solution)/shard_map/slice | solution.py:142
  294.4 12.5 %copy.88 = f32[6,64,720]{2,1,0:T(8,128)S(1)} copy(f32[6,64,720]{0,2,1:T(8,128)} %bitcast.41) | data formatting | bytes 2211840 | tf_op jit(solution)/shard_map/reshape | solution.py:140
  307.0 7.7 %collective-permute-start.11 = (f32[6,1,720]{2,1,0:T(1,128)S(1)}, f32[6,1,720]{2,1,0:T(1,128)S(1)}, u32[]{:S(2)}, u32[]{:S(2)}) collective-permute-start(f32[6,1,720]{2,1,0:T(1,128)S(1)} %get-tuple-element.46), channel_id=1, source_target_pairs={{0,8},{8,16},{16,24},{24,32},{32,40},{40,48},{48,56},{56,64},{64,7... | collective-permute-start | bytes 51848 | tf_op jit(solution)/shard_map/ppermute | solution.py:17
  321.1 4.0 collective-permute-start.13
  325.3 3.8 collective-permute-done.12
  333.6 77.1 %all-reduce.3.cloned.1.call-done = f32[360,128]{1,0:T(8,128)} async-done(((f32[360,128]{1,0:T(8,128)}), f32[360,128]{1,0:T(8,128)}) %all-reduce.3.cloned.1.call-update) | async-done | bytes 184336 | tf_op jit(solution)/shard_map/psum | solution.py:34
  410.8 9.0 %collective-permute-start.15 = (f32[6,1,720]{2,1,0:T(1,128)S(1)}, f32[6,1,720]{2,1,0:T(1,128)S(1)}, u32[]{:S(2)}, u32[]{:S(2)}) collective-permute-start(f32[6,1,720]{2,1,0:T(1,128)S(1)} %get-tuple-element.40), channel_id=1, source_target_pairs={{0,8},{8,16},{16,24},{24,32},{32,40},{40,48},{48,56},{56,64},{64,7... | collective-permute-start | bytes 51848 | tf_op jit(solution)/shard_map/ppermute | solution.py:17
  426.3 4.2 collective-permute-start.17
  430.6 5.8 %collective-permute-done.16 = f32[1,66,720]{2,1,0:T(8,128)S(1)} collective-permute-done((f32[1,66,720]{2,1,0:T(8,128)S(1)}, f32[1,66,720]{2,1,0:T(8,128)S(1)}, u32[]{:S(2)}, u32[]{:S(2)}) %collective-permute-start.16) | collective-permute-done | bytes 190112 | tf_op jit(solution)/shard_map/ppermute | solution.py:19
  436.4 3.3 fusion.7
  439.7 45.7 %all-gather.4.cloned.1.call-done = f32[11520,128]{1,0:T(8,128)} async-done(((f32[360,128]{1,0:T(8,128)}), f32[11520,128]{1,0:T(8,128)}) %all-gather.4.cloned.1.call-update) | async-done | bytes 5898256 | tf_op jit(solution)/shard_map/all_gather | solution.py:144
  485.4 3.3 gather_fusion.1
  488.8 7.0 %fusion.76 = f32[90,1,128]{2,1,0:T(1,128)S(1)} fusion(f32[90,128,128]{2,1,0:T(8,128)} %param.23, f32[90,128,1]{1,0,2:T(8,128)S(1)} %select_bitcast_fusion), kind=kOutput, calls=%fused_computation.147 | convolution fusion | flops 17694720 | bytes 5990400 | tf_op jit(solution)/shard_map/ecf,ec->ef/dot_general | solution.py:150
  (164 shorter events, 50.0 us)
Async XLA Ops:
  7.2 126.8 %reduce-scatter.4.cloned.1.call-start = ((), (), s32[]{:S(2)}) async-start(), calls=%async_computation.4 | async-start | bytes 6082560
  27.9 106.2 %copy-start.10 = (f32[6,64,720]{2,1,0:T(8,128)S(1)}, f32[6,64,720]{2,1,0:T(8,128)}, u32[]{:S(2)}) copy-start(f32[6,64,720]{2,1,0:T(8,128)} %param.19) | copy-start | bytes 3317764
  27.9 158.8 %all-gather.6.cloned.1.call-start = ((), (), s32[]{:S(2)}) async-start(), calls=%async_computation.3 | async-start | bytes 1658880 | tf_op jit(solution)/shard_map/all_gather | solution.py:114
  29.7 115.1 %collective-permute-start.1 = (f32[6,1,720]{2,1,0:T(1,128)}, f32[6,1,720]{2,1,0:T(1,128)}, u32[]{:S(2)}, u32[]{:S(2)}) collective-permute-start(f32[6,1,720]{2,1,0:T(1,128)} %get-tuple-element.58), channel_id=1, source_target_pairs={{0,8},{8,16},{16,24},{24,32},{32,40},{40,48},{48,56},{56,64},{64,7... | collective-permute-start | bytes 51848 | tf_op jit(solution)/shard_map/ppermute | solution.py:17
  34.3 110.5 %collective-permute-start.2 = (f32[6,1,720]{2,1,0:T(1,128)}, f32[6,1,720]{2,1,0:T(1,128)}, u32[]{:S(2)}, u32[]{:S(2)}) collective-permute-start(f32[6,1,720]{2,1,0:T(1,128)} %get-tuple-element.59), channel_id=1, source_target_pairs={{8,0},{16,8},{24,16},{32,24},{40,32},{48,40},{56,48},{64,56},{72,6... | collective-permute-start | bytes 51848 | tf_op jit(solution)/shard_map/ppermute | solution.py:19
  134.1 276.7 %all-reduce.3.cloned.1.call-start = ((), (), s32[]{:S(2)}) async-start(), calls=%async_computation.1 | async-start | bytes 368640 | tf_op jit(solution)/shard_map/psum | solution.py:34
  134.3 77.3 %copy-start.3 = (f32[6,64,720]{2,1,0:T(8,128)}, f32[6,64,720]{2,1,0:T(8,128)S(1)}, u32[]{:S(2)}) copy-start(f32[6,64,720]{2,1,0:T(8,128)S(1)} %broadcast_select_fusion.1) | copy-start | bytes 3317764
  134.3 20.0 %collective-permute-start = (f32[6,720]{1,0:T(8,128)S(1)}, f32[6,720]{1,0:T(8,128)S(1)}, u32[]{:S(2)}, u32[]{:S(2)}) collective-permute-start(f32[6,720]{1,0:T(8,128)S(1)} %bitcast.58), channel_id=1, source_target_pairs={{0,8},{8,16},{16,24},{24,32},{32,40},{40,48},{48,56},{56,64},{64,7... | collective-permute-start | bytes 51848 | tf_op jit(solution)/shard_map/ppermute | solution.py:29
  139.6 14.7 %collective-permute-start.4 = (f32[64,720]{1,0:T(8,128)}, f32[64,720]{1,0:T(8,128)S(1)}, u32[]{:S(2)}, u32[]{:S(2)}) collective-permute-start(f32[64,720]{1,0:T(8,128)} %slice_bitcast_fusion), channel_id=1, source_target_pairs={{0,1},{1,2},{2,3},{3,4},{4,5},{5,6},{6,7},{8,9},{9,10},{10,11},{11... | collective-permute-start | bytes 552968 | tf_op jit(solution)/shard_map/ppermute | solution.py:29
  145.6 15.2 %collective-permute-start.3 = (f32[1,66,720]{2,1,0:T(8,128)S(1)}, f32[1,66,720]{2,1,0:T(8,128)S(1)}, u32[]{:S(2)}, u32[]{:S(2)}) collective-permute-start(f32[1,66,720]{2,1,0:T(8,128)S(1)} %get-tuple-element.34), channel_id=1, source_target_pairs={{1,0},{2,1},{3,2},{4,3},{5,4},{6,5},{7,6},{9,8},{10,9},{11,10},{12... | collective-permute-start | bytes 570248 | tf_op jit(solution)/shard_map/ppermute | solution.py:19
  147.0 14.7 %collective-permute-start.5 = (f32[1,66,720]{2,1,0:T(8,128)S(1)}, f32[1,66,720]{2,1,0:T(8,128)S(1)}, u32[]{:S(2)}, u32[]{:S(2)}) collective-permute-start(f32[1,66,720]{2,1,0:T(8,128)S(1)} %get-tuple-element.35), channel_id=1, source_target_pairs={{0,1},{1,2},{2,3},{3,4},{4,5},{5,6},{6,7},{8,9},{9,10},{10,11},{11... | collective-permute-start | bytes 570248 | tf_op jit(solution)/shard_map/ppermute | solution.py:17
  193.3 6.3 %collective-permute-start.6 = (f32[6,1,720]{2,1,0:T(1,128)S(1)}, f32[6,1,720]{2,1,0:T(1,128)S(1)}, u32[]{:S(2)}, u32[]{:S(2)}) collective-permute-start(f32[6,1,720]{2,1,0:T(1,128)S(1)} %get-tuple-element.52), channel_id=1, source_target_pairs={{0,8},{8,16},{16,24},{24,32},{32,40},{40,48},{48,56},{56,64},{64,7... | collective-permute-start | bytes 51848 | tf_op jit(solution)/shard_map/ppermute | solution.py:17
  197.1 5.1 %collective-permute-start.7 = (f32[6,1,720]{2,1,0:T(1,128)S(1)}, f32[6,1,720]{2,1,0:T(1,128)S(1)}, u32[]{:S(2)}, u32[]{:S(2)}) collective-permute-start(f32[6,1,720]{2,1,0:T(1,128)S(1)} %get-tuple-element.53), channel_id=1, source_target_pairs={{8,0},{16,8},{24,16},{32,24},{40,32},{48,40},{56,48},{64,56},{72,6... | collective-permute-start | bytes 51848 | tf_op jit(solution)/shard_map/ppermute | solution.py:19
  202.3 9.0 %collective-permute-start.8 = (f32[1,66,720]{2,1,0:T(8,128)S(1)}, f32[1,66,720]{2,1,0:T(8,128)S(1)}, u32[]{:S(2)}, u32[]{:S(2)}) collective-permute-start(f32[1,66,720]{2,1,0:T(8,128)S(1)} %get-tuple-element.32), channel_id=1, source_target_pairs={{1,0},{2,1},{3,2},{4,3},{5,4},{6,5},{7,6},{9,8},{10,9},{11,10},{12... | collective-permute-start | bytes 570248 | tf_op jit(solution)/shard_map/ppermute | solution.py:19
  203.6 8.0 %collective-permute-start.9 = (f32[1,66,720]{2,1,0:T(8,128)S(1)}, f32[1,66,720]{2,1,0:T(8,128)S(1)}, u32[]{:S(2)}, u32[]{:S(2)}) collective-permute-start(f32[1,66,720]{2,1,0:T(8,128)S(1)} %get-tuple-element.33), channel_id=1, source_target_pairs={{0,1},{1,2},{2,3},{3,4},{4,5},{5,6},{6,7},{8,9},{9,10},{10,11},{11... | collective-permute-start | bytes 570248 | tf_op jit(solution)/shard_map/ppermute | solution.py:17
  228.7 31.9 %copy-start.34 = (f32[2048]{0:T(1024)S(1)}, f32[2048]{0:T(1024)}, u32[]{:S(2)}) copy-start(f32[2048]{0:T(1024)} %param.31) | copy-start | bytes 24580
  228.8 31.9 %copy-start.35 = (f32[2048]{0:T(1024)S(1)}, f32[2048]{0:T(1024)}, u32[]{:S(2)}) copy-start(f32[2048]{0:T(1024)} %param.30) | copy-start | bytes 24580
  307.0 10.2 %collective-permute-start.11 = (f32[6,1,720]{2,1,0:T(1,128)S(1)}, f32[6,1,720]{2,1,0:T(1,128)S(1)}, u32[]{:S(2)}, u32[]{:S(2)}) collective-permute-start(f32[6,1,720]{2,1,0:T(1,128)S(1)} %get-tuple-element.46), channel_id=1, source_target_pairs={{0,8},{8,16},{16,24},{24,32},{32,40},{40,48},{48,56},{56,64},{64,7... | collective-permute-start | bytes 51848 | tf_op jit(solution)/shard_map/ppermute | solution.py:17
  314.7 5.1 %collective-permute-start.10 = (f32[6,1,720]{2,1,0:T(1,128)S(1)}, f32[6,1,720]{2,1,0:T(1,128)S(1)}, u32[]{:S(2)}, u32[]{:S(2)}) collective-permute-start(f32[6,1,720]{2,1,0:T(1,128)S(1)} %get-tuple-element.47), channel_id=1, source_target_pairs={{8,0},{16,8},{24,16},{32,24},{40,32},{48,40},{56,48},{64,56},{72,6... | collective-permute-start | bytes 51848 | tf_op jit(solution)/shard_map/ppermute | solution.py:19
  319.8 9.2 %collective-permute-start.12 = (f32[1,66,720]{2,1,0:T(8,128)S(1)}, f32[1,66,720]{2,1,0:T(8,128)S(1)}, u32[]{:S(2)}, u32[]{:S(2)}) collective-permute-start(f32[1,66,720]{2,1,0:T(8,128)S(1)} %get-tuple-element.30), channel_id=1, source_target_pairs={{1,0},{2,1},{3,2},{4,3},{5,4},{6,5},{7,6},{9,8},{10,9},{11,10},{12... | collective-permute-start | bytes 570248 | tf_op jit(solution)/shard_map/ppermute | solution.py:19
  321.1 8.0 %collective-permute-start.13 = (f32[1,66,720]{2,1,0:T(8,128)S(1)}, f32[1,66,720]{2,1,0:T(8,128)S(1)}, u32[]{:S(2)}, u32[]{:S(2)}) collective-permute-start(f32[1,66,720]{2,1,0:T(8,128)S(1)} %get-tuple-element.31), channel_id=1, source_target_pairs={{0,1},{1,2},{2,3},{3,4},{4,5},{5,6},{6,7},{8,9},{9,10},{10,11},{11... | collective-permute-start | bytes 570248 | tf_op jit(solution)/shard_map/ppermute | solution.py:17
  331.7 79.1 %copy-start.37 = (s32[90]{0:T(128)S(1)}, s32[90]{0:T(128)}, u32[]{:S(2)}) copy-start(s32[90]{0:T(128)} %get-tuple-element.65) | copy-start | bytes 1084
  331.7 79.1 %copy-start.38 = (s32[90]{0:T(128)S(1)}, s32[90]{0:T(128)}, u32[]{:S(2)}) copy-start(s32[90]{0:T(128)} %param.25) | copy-start | bytes 1084
  331.7 79.1 %copy-start.39 = (s32[90,1]{0,1:T(1,128)S(1)}, s32[90,1]{0,1:T(1,128)}, u32[]{:S(2)}) copy-start(s32[90,1]{0,1:T(1,128)} %param.24) | copy-start | bytes 1084
  333.5 151.9 %all-gather.4.cloned.1.call-start = ((), (), s32[]{:S(2)}) async-start(), calls=%async_computation.2 | async-start | bytes 6082560 | tf_op jit(solution)/shard_map/all_gather | solution.py:144
  410.8 11.4 %collective-permute-start.15 = (f32[6,1,720]{2,1,0:T(1,128)S(1)}, f32[6,1,720]{2,1,0:T(1,128)S(1)}, u32[]{:S(2)}, u32[]{:S(2)}) collective-permute-start(f32[6,1,720]{2,1,0:T(1,128)S(1)} %get-tuple-element.40), channel_id=1, source_target_pairs={{0,8},{8,16},{16,24},{24,32},{32,40},{40,48},{48,56},{56,64},{64,7... | collective-permute-start | bytes 51848 | tf_op jit(solution)/shard_map/ppermute | solution.py:17
  419.8 5.1 %collective-permute-start.14 = (f32[6,1,720]{2,1,0:T(1,128)S(1)}, f32[6,1,720]{2,1,0:T(1,128)S(1)}, u32[]{:S(2)}, u32[]{:S(2)}) collective-permute-start(f32[6,1,720]{2,1,0:T(1,128)S(1)} %get-tuple-element.41), channel_id=1, source_target_pairs={{8,0},{16,8},{24,16},{32,24},{40,32},{48,40},{56,48},{64,56},{72,6... | collective-permute-start | bytes 51848 | tf_op jit(solution)/shard_map/ppermute | solution.py:19
  421.8 14.6 %copy-start.13 = (f32[6,64,720]{2,1,0:T(8,128)S(1)}, f32[6,64,720]{2,1,0:T(8,128)}, u32[]{:S(2)}) copy-start(f32[6,64,720]{2,1,0:T(8,128)} %param.19) | copy-start | bytes 3317764
  421.8 14.6 %copy-start.16 = (f32[5,64,720]{2,1,0:T(8,128)S(1)}, f32[5,64,720]{2,1,0:T(8,128)}, u32[]{:S(2)}) copy-start(f32[5,64,720]{2,1,0:T(8,128)} %slice.302) | copy-start | bytes 2764804
  421.8 14.6 %copy-start.21 = (f32[6,64,1]{2,1,0:T(8,128)S(1)}, f32[6,64,1]{2,1,0:T(8,128)}, u32[]{:S(2)}) copy-start(f32[6,64,1]{2,1,0:T(8,128)} %copy-done.18) | copy-start | bytes 4612
  425.0 11.4 %collective-permute-start.16 = (f32[1,66,720]{2,1,0:T(8,128)S(1)}, f32[1,66,720]{2,1,0:T(8,128)S(1)}, u32[]{:S(2)}, u32[]{:S(2)}) collective-permute-start(f32[1,66,720]{2,1,0:T(8,128)S(1)} %get-tuple-element.28), channel_id=1, source_target_pairs={{1,0},{2,1},{3,2},{4,3},{5,4},{6,5},{7,6},{9,8},{10,9},{11,10},{12... | collective-permute-start | bytes 570248 | tf_op jit(solution)/shard_map/ppermute | solution.py:19
  426.3 10.1 %collective-permute-start.17 = (f32[1,66,720]{2,1,0:T(8,128)S(1)}, f32[1,66,720]{2,1,0:T(8,128)S(1)}, u32[]{:S(2)}, u32[]{:S(2)}) collective-permute-start(f32[1,66,720]{2,1,0:T(8,128)S(1)} %get-tuple-element.29), channel_id=1, source_target_pairs={{0,1},{1,2},{2,3},{3,4},{4,5},{5,6},{6,7},{8,9},{9,10},{10,11},{11... | collective-permute-start | bytes 570248 | tf_op jit(solution)/shard_map/ppermute | solution.py:17
  (32 other events, 313.2 us)
Sparse Core Ops, SparseCore 0:
  28.1 105.9 reduce-scatter.3
  135.8 50.8 all-gather.5
  333.7 77.0 all-reduce.2
  413.2 72.1 all-gather.3
